TPU v7x, 128 devices: a whole 4x4x4 slice. The times are simulated.
128 devices in a mesh: row: 32 (over y, z, core), col: 4 (over x).
Axes of the slice: x: 4, y: 4, z: 4, core: 2. Of those that a mesh axis runs over, the one named last changes fastest.
Arguments:
- amplitudes: bfloat16 [4, 1280, 1280], P(None, ('row', 'col')), may hold values from -0.75 to 0.75
- integrals: bfloat16 [96, 1280, 1280], P('row', 'col'), may hold values from -0.15625 to 0.15625
- occupied_integrals: bfloat16 [96, 160, 1280], P('row'), may hold values from -1 to 1
- pair_orbitals: int32 [4, 2], replicated, may hold values from 0 to 159
- amplitude_tiles: int32 [4, 20, 20], replicated, may hold values 0 or 1
- integral_tiles: int32 [20, 20], replicated, may hold values 0 or 1
Outputs:
- residual: float32 [4, 1280, 1280], P(None, 'col', 'row')
All inputs are finite; a program needn't handle non-finite values.
Results may differ from a plain program's by a relative error of at most 0.005.
Values may be sent and summed in bfloat16 or wider, within the bound.
A program may use at most 128 MiB of HBM per device.

v0:
```python
import jax
import jax.numpy as jnp
from jax import lax
from jax.sharding import PartitionSpec as P

TILE = 64


def mask_rows(amp_rows, amp_tiles, tile_size):
    row_count = amp_rows.shape[1]
    tile_count = amp_tiles.shape[1]
    tile_of = jnp.arange(row_count, dtype=jnp.int32) // tile_size
    picker = (tile_of[:, None] == jnp.arange(tile_count, dtype=jnp.int32)[None, :]).astype(
        jnp.float32
    )
    row_mask = jnp.einsum("nk,pkm->pnm", picker, amp_tiles.astype(jnp.float32))
    row_mask = jnp.repeat(row_mask, tile_size, axis=2)
    return amp_rows * row_mask.astype(amp_rows.dtype)


def local(
    amplitudes, integrals, occupied_integrals, pair_orbitals, amplitude_tiles, integral_tiles
):
    column_index = lax.axis_index("col")
    local_rows = integrals.shape[1]
    tiles_here = local_rows // TILE
    tile_rows = lax.dynamic_slice_in_dim(integral_tiles, column_index * tiles_here, tiles_here, 0)
    factor_mask = jnp.repeat(jnp.repeat(tile_rows, TILE, axis=0), TILE, axis=1)
    masked_int = integrals * factor_mask.astype(jnp.bfloat16)[None]
    orbital_ids = jnp.arange(occupied_integrals.shape[1], dtype=jnp.int32)
    pick_first = (pair_orbitals[:, 0][:, None] == orbital_ids[None, :]).astype(jnp.bfloat16)
    pick_second = (pair_orbitals[:, 1][:, None] == orbital_ids[None, :]).astype(jnp.bfloat16)
    first_rows = jnp.einsum(
        "po,qov->qpv", pick_first, occupied_integrals, preferred_element_type=jnp.float32
    )
    second_rows = jnp.einsum(
        "po,qov->qpv", pick_second, occupied_integrals, preferred_element_type=jnp.float32
    ).astype(jnp.bfloat16)
    whole_amp = lax.all_gather(amplitudes, ("row", "col"), axis=1, tiled=True)
    masked_amp = mask_rows(whole_amp, amplitude_tiles, TILE)
    inter = jnp.einsum(
        "qac,pcd->qpad", masked_int, masked_amp, preferred_element_type=jnp.float32
    ).astype(jnp.bfloat16)
    carried = jnp.einsum(
        "qpc,pcd->qpd", second_rows, masked_amp, preferred_element_type=jnp.float32
    )
    first_here = lax.dynamic_slice_in_dim(first_rows, column_index * local_rows, local_rows, 2)
    ladder = jnp.einsum(
        "qpad,qbd->pab",
        inter,
        lax.all_gather(masked_int, "col", axis=1, tiled=True),
        preferred_element_type=jnp.float32,
    )
    cycle = jnp.einsum("qpa,qpb->pab", first_here, carried)
    return lax.psum_scatter(ladder + cycle, "row", scatter_dimension=2, tiled=True)


def solution(mesh):
    placed = (
        P(None, ("row", "col"), None),
        P("row", "col", None),
        P("row", None, None),
        P(),
        P(),
        P(),
    )
    return jax.shard_map(
        local, mesh=mesh, in_specs=placed, out_specs=P(None, "col", "row"), check_vma=False
    )
```

profile of v0, /device:TPU:0, one launch (start us, length us, event | category | flops | bytes accessed | tf_op | source)
XLA Modules:
  0.0 317.9 jit_solution(4331648339381374294)
XLA Ops:
  6.5 0.7 all-gather.3.cloned.1.call-update
  7.3 0.0 all-gather.5.cloned.1.call-start
  7.3 0.7 dynamic-slice_convert_fusion
  8.0 0.1 copy.23
  8.1 0.1 broadcast_in_dim.7
  8.2 0.1 convert_element_type.48
  8.3 0.1 broadcast_in_dim.16
  8.4 0.6 copy.24
  9.0 3.4 %broadcast_multiply_fusion = bf16[3,320,1280]{2,1,0:T(8,128)(2,1)} fusion(bf16[3,320,1280]{2,1,0:T(8,128)(2,1)} %param.7, bf16[320,1280]{1,0:T(8,128)(2,1)S(1)} %copy.24), kind=kLoop, calls=%fused_computation.13 | loop fusion | flops 1228800 | bytes 5734400 | tf_op jit(solution)/shard_map/mul | solution.py:29
  12.5 0.0 all-gather.5.cloned.1.call-update
  12.5 0.0 reduce-scatter.2.cloned.1.call-start
  12.6 0.3 fusion.20
  12.9 0.1 dynamic-slice_bitcast_fusion
  13.0 0.3 fusion.7
  13.3 0.3 fusion.8
  13.6 73.3 %all-gather.3.cloned.1.call-done = bf16[4,1280,1280]{2,0,1:T(4,128)(2,1)} async-done(((bf16[4,10,1280]{2,0,1:T(4,128)(2,1)}), bf16[4,1280,1280]{2,0,1:T(4,128)(2,1)}) %all-gather.3.cloned.1.call-update) | async-done | bytes 13107216 | tf_op jit(solution)/shard_map/all_gather | solution.py:39
  87.0 21.2 %copy.22 = bf16[4,1280,1280]{1,2,0:T(8,128)(2,1)} copy(bf16[4,1280,1280]{2,0,1:T(4,128)(2,1)} %all-gather.3.cloned.1.call-done) | data formatting | bytes 26214400 | tf_op jit(solution)/shard_map/all_gather | solution.py:39
  108.2 6.3 %bitcast_multiply_fusion = bf16[4,1280,1280]{1,2,0:T(8,128)(2,1)S(1)} fusion(bf16[4,1280,1280]{1,2,0:T(8,128)(2,1)} %copy.22, bf16[4,1280,20]{1,2,0:T(8,128)(2,1)S(1)} %fusion.7), kind=kLoop, calls=%fused_computation.2 | loop fusion | flops 6553600 | bytes 26419200 | tf_op jit(solution)/shard_map/mul | solution.py:18
  114.6 4.7 %copy-done.2 = bf16[4,1280,1280]{1,2,0:T(8,128)(2,1)} copy-done((bf16[4,1280,1280]{1,2,0:T(8,128)(2,1)}, bf16[4,1280,1280]{1,2,0:T(8,128)(2,1)S(1)}, u32[]{:S(2)}) %copy-start.2) | copy-done | bytes 13107224
  119.3 15.0 %fusion.1 = bf16[3,4,320,1280]{3,2,0,1:T(8,128)(2,1)} fusion(bf16[4,1280,1280]{1,2,0:T(8,128)(2,1)S(1)} %bitcast_multiply_fusion, bf16[3,320,1280]{2,1,0:T(8,128)(2,1)S(1)} %copy-done.3), kind=kOutput, calls=%fused_computation.3 | convolution fusion | flops 12587827200 | bytes 25395200 | tf_op jit(solution)/shard_map/qac,pcd->qpad/dot_general | solution.py:41
  134.3 49.2 %all-gather.5.cloned.1.call-done = bf16[3,1280,1280]{2,1,0:T(8,128)(2,1)} async-done(((bf16[3,320,1280]{2,1,0:T(8,128)(2,1)}), bf16[3,1280,1280]{2,1,0:T(8,128)(2,1)}) %all-gather.5.cloned.1.call-update) | async-done | bytes 9830416 | tf_op jit(solution)/shard_map/all_gather | solution.py:51
  183.4 21.9 %fusion.4 = f32[4,320,1280,1]{1,2,3,0:T(8,128)} fusion(bf16[3,4,320,1280]{3,2,0,1:T(8,128)(2,1)} %fusion.1, bf16[3,1280,1280]{2,1,0:T(8,128)(2,1)} %all-gather.5.cloned.1.call-done), kind=kOutput, calls=%fused_computation.4 | convolution fusion | flops 12582912000 | bytes 26214400 | tf_op jit(solution)/shard_map/qpad,qbd->pab/dot_general | solution.py:48
  205.3 14.8 %bitcast_add_fusion = f32[4,320,1280]{1,2,0:T(8,128)} fusion(f32[4,320,1280,1]{1,2,3,0:T(8,128)} %fusion.4, bf16[4,1280,1280]{1,2,0:T(8,128)(2,1)} %copy-done.2, bf16[3,4,1280]{2,1,0:T(4,128)(2,1)S(1)} %fusion.8, bf16[3,4,320]{2,1,0:T(4,128)(2,1)S(1)} %dynamic-slice_bitcast_fusion), kind=kOutput, calls=%fused_computation.6 | convolution fusion | flops 50790400 | bytes 26252800 | tf_op jit(solution)/shard_map/qpa,qpb->pab/dot_general | solution.py:54
  220.1 91.3 %reduce-scatter.2.cloned.1.call-done = f32[4,320,40]{1,2,0:T(8,128)} async-done(((f32[4,320,1280]{1,2,0:T(8,128)}), f32[4,320,40]{1,2,0:T(8,128)}) %reduce-scatter.2.cloned.1.call-update) | async-done | bytes 204816 | tf_op jit(solution)/shard_map/reduce_scatter | solution.py:55
  (16 shorter events, 0.1 us)
Async XLA Ops:
  6.5 6.1 %copy-start = (bf16[3,160,1280]{2,1,0:T(8,128)(2,1)S(1)}, bf16[3,160,1280]{2,1,0:T(8,128)(2,1)}, u32[]{:S(2)}) copy-start(bf16[3,160,1280]{2,1,0:T(8,128)(2,1)} %param.8) | copy-start | bytes 3686404
  6.5 6.0 %copy-start.4 = (s32[4,20,20]{2,0,1:T(4,128)S(1)}, s32[4,20,20]{2,0,1:T(4,128)}, u32[]{:S(2)}) copy-start(s32[4,20,20]{2,0,1:T(4,128)} %param.10) | copy-start | bytes 19204
  6.5 6.1 %copy-start.5 = (s32[4,2]{0,1:T(2,128)S(1)}, s32[4,2]{0,1:T(2,128)}, u32[]{:S(2)}) copy-start(s32[4,2]{0,1:T(2,128)} %param.9) | copy-start | bytes 100
  6.5 80.5 %all-gather.3.cloned.1.call-start = ((), (), s32[]{:S(2)}) async-start(), calls=%async_computation.1 | async-start | bytes 13209600 | tf_op jit(solution)/shard_map/all_gather | solution.py:39
  7.3 176.2 %all-gather.5.cloned.1.call-start = ((), (), s32[]{:S(2)}) async-start(), calls=%async_computation.2 | async-start | bytes 12288000 | tf_op jit(solution)/shard_map/all_gather | solution.py:51
  12.5 298.9 %reduce-scatter.2.cloned.1.call-start = ((), (), s32[]{:S(2)}) async-start(), calls=%async_computation.3 | async-start | bytes 8110080 | tf_op jit(solution)/shard_map/reduce_scatter | solution.py:55
  108.2 11.0 %copy-start.3 = (bf16[3,320,1280]{2,1,0:T(8,128)(2,1)S(1)}, bf16[3,320,1280]{2,1,0:T(8,128)(2,1)}, u32[]{:S(2)}) copy-start(bf16[3,320,1280]{2,1,0:T(8,128)(2,1)} %broadcast_multiply_fusion) | copy-start | bytes 7372804
  114.6 4.7 %copy-start.2 = (bf16[4,1280,1280]{1,2,0:T(8,128)(2,1)}, bf16[4,1280,1280]{1,2,0:T(8,128)(2,1)S(1)}, u32[]{:S(2)}) copy-start(bf16[4,1280,1280]{1,2,0:T(8,128)(2,1)S(1)} %bitcast_multiply_fusion) | copy-start | bytes 39321604
  205.3 106.1 %copy-start.1 = (bf16[3,160,1280]{2,1,0:T(8,128)(2,1)S(1)}, bf16[3,160,1280]{2,1,0:T(8,128)(2,1)}, u32[]{:S(2)}) copy-start(bf16[3,160,1280]{2,1,0:T(8,128)(2,1)} %param.8) | copy-start | bytes 3686404
Sparse Core Ops, SparseCore 0:
  10.3 76.6 all-gather.2
  88.7 94.7 all-gather.4
  220.2 91.0 reduce-scatter.1
where the time goes:
time: 319 us; the launch traced here: 318 us
  waiting for transfers between devices  215 us (67%)
  matrix products  52.6 us (16%)
  local copies, waits for them, and re-layouts  27 us (8%)
  between operations  13.2 us (4%)
  other arithmetic  10.5 us (3%)
    reduce_scatter x1, waiting for transfers between devices, local(): lax.psum_scatter(ladder + cycle, 'row', scatter_dimension=2, tiled=True)  91.3 us
    all_gather x1, waiting for transfers between devices, local(): whole_amp = lax.all_gather(amplitudes, ('row', 'col'), axis=1, tiled=True)  73.3 us
    all_gather x1, waiting for transfers between devices, local(): lax.all_gather(masked_int, 'col', axis=1, tiled=True)  49.2 us
    dot_general x1, matrix products, local(): jnp.einsum('qpad,qbd->pab', inter, lax.all_gather(masked_int, 'col', axis...  21.9 us
    all_gather x1, local copies, waits for them, and re-layouts, local(): whole_amp = lax.all_gather(amplitudes, ('row', 'col'), axis=1, tiled=True)  21.2 us
    dot_general x1, matrix products, local(): jnp.einsum('qac,pcd->qpad', masked_int, masked_amp, preferred_element_typ...  15 us
    dot_general x1, matrix products, local(): cycle = jnp.einsum('qpa,qpb->pab', first_here, carried)  14.8 us
  transfers between devices with their start and end apart: 3, of which 3 were waited for; matrix products, arithmetic and copies ran while one was open for 15% of the time, Pallas kernels for 0%

commit v1 on v0

--- a/solution.py
+++ b/solution.py
@@ -48,7 +48,9 @@
     ladder = jnp.einsum(
         "qpad,qbd->pab",
         inter,
-        lax.all_gather(masked_int, "col", axis=1, tiled=True),
+        jnp.concatenate(
+            lax.all_to_all(jnp.stack([masked_int] * lax.axis_size("col")), "col", 0, 0), axis=1
+        ),
         preferred_element_type=jnp.float32,
     )
     cycle = jnp.einsum("qpa,qpb->pab", first_here, carried)

time: 319 us -> 341 us (1.069)
  local copies, waits for them, and re-layouts: 27 us -> 36.3 us
  waiting for transfers between devices: 215 us -> 222 us
  starting transfers between devices: 0.08 us -> 6.1 us
    all_to_all x0 -> x1, waiting for transfers between devices: none -> 131 us  [local(): lax.all_to_all(jnp.stack([masked_int] * lax.axis_size('col')), 'col', 0, 0)]
    all_gather x1, waiting for transfers between devices: 73.3 us -> 0.01 us  [local(): whole_amp = lax.all_gather(amplitudes, ('row', 'col'), axis=1, tiled=True)]
    all_gather x1 -> x0, waiting for transfers between devices: 49.2 us -> none  [local(): lax.all_gather(masked_int, 'col', axis=1, tiled=True)]
    reshape x0 -> x1, local copies, waits for them, and re-layouts: none -> 8.22 us  [local(): jnp.concatenate(lax.all_to_all(jnp.stack([masked_int] * lax.axis_size('co...]
    all_to_all x0 -> x1, starting transfers between devices: none -> 6.06 us  [local(): lax.all_to_all(jnp.stack([masked_int] * lax.axis_size('col')), 'col', 0, 0)]
    another operation x0 -> x1, local copies, waits for them, and re-layouts: none -> 4.69 us  [local(): jnp.stack([masked_int] * lax.axis_size('col'))]
  transfers between devices with their start and end apart: 3 -> 3, of which waited for: 3 -> 2; matrix products, arithmetic and copies ran while one was open for 15% -> 5% of each run, Pallas kernels for 0% -> 0%
where the time goes in v1:
time: 341 us; the launch traced here: 340 us
  waiting for transfers between devices  222 us (65%)
  matrix products  52.6 us (15%)
  local copies, waits for them, and re-layouts  36.3 us (11%)
  between operations  13.5 us (4%)
  other arithmetic  8.95 us (3%)
  starting transfers between devices  6.1 us (2%)
    all_to_all x1, waiting for transfers between devices, local(): lax.all_to_all(jnp.stack([masked_int] * lax.axis_size('col')), 'col', 0, 0)  131 us
    reduce_scatter x1, waiting for transfers between devices, local(): lax.psum_scatter(ladder + cycle, 'row', scatter_dimension=2, tiled=True)  90.7 us
    dot_general x1, matrix products, local(): jnp.einsum('qpad,qbd->pab', inter, jnp.concatenate(lax.all_to_all(jnp.sta...  21.9 us
    all_gather x1, local copies, waits for them, and re-layouts, local(): whole_amp = lax.all_gather(amplitudes, ('row', 'col'), axis=1, tiled=True)  20.9 us
    dot_general x1, matrix products, local(): jnp.einsum('qac,pcd->qpad', masked_int, masked_amp, preferred_element_typ...  15 us
    dot_general x1, matrix products, local(): cycle = jnp.einsum('qpa,qpb->pab', first_here, carried)  14.8 us
    reshape x1, local copies, waits for them, and re-layouts, local(): jnp.concatenate(lax.all_to_all(jnp.stack([masked_int] * lax.axis_size('co...  8.22 us
  transfers between devices with their start and end apart: 3, of which 2 were waited for; matrix products, arithmetic and copies ran while one was open for 5% of the time, Pallas kernels for 0%

profile of v1, /device:TPU:0, one launch (start us, length us, event | category | flops | bytes accessed | tf_op | source)
XLA Modules:
  0.0 340.0 jit_solution(11305332592900037119)
XLA Ops:
  6.5 0.7 all-gather.2.cloned.1.call-update
  7.3 0.7 dynamic-slice_convert_fusion
  8.0 0.1 copy.23
  8.1 0.1 broadcast_in_dim.7
  8.2 0.1 convert_element_type.48
  8.3 0.1 broadcast_in_dim.16
  8.4 0.6 copy.24
  9.0 1.9 broadcast_multiply_fusion
  10.9 1.4 copy-done.3
  12.3 4.7 %stack.2 = bf16[4,3,320,1280]{3,2,1,0:T(8,128)(2,1)} broadcast(bf16[3,320,1280]{2,1,0:T(8,128)(2,1)S(1)} %broadcast_multiply_fusion), dimensions={1,2,3} | broadcast | bytes 12288000 | tf_op jit(solution)/shard_map/stack | solution.py:52
  17.0 6.1 %all-to-all-start = ((bf16[4,3,320,1280]{3,2,1,0:T(8,128)(2,1)}), bf16[4,3,320,1280]{3,2,1,0:T(8,128)(2,1)}, u32[]{:S(2)}, u32[]{:S(2)}) async-start(bf16[4,3,320,1280]{3,2,1,0:T(8,128)(2,1)} %stack.2), calls=%async_computation | async-start | bytes 19660800 | tf_op jit(solution)/shard_map/all_to_all | solution.py:52
  23.1 0.0 reduce-scatter.2.cloned.1.call-start
  23.2 0.3 fusion.23
  23.5 0.1 dynamic-slice_bitcast_fusion
  23.6 0.3 fusion.10
  23.9 0.3 fusion.11
  24.2 131.1 %all-to-all-done = bf16[4,3,320,1280]{3,2,1,0:T(8,128)(2,1)} async-done(((bf16[4,3,320,1280]{3,2,1,0:T(8,128)(2,1)}), bf16[4,3,320,1280]{3,2,1,0:T(8,128)(2,1)}, u32[]{:S(2)}, u32[]{:S(2)}) %all-to-all-start) | async-done | bytes 9830432 | tf_op jit(solution)/shard_map/all_to_all | solution.py:52
  155.3 8.2 %copy.26 = bf16[3,4,320,1280]{3,2,1,0:T(8,128)(2,1)} copy(bf16[3,4,320,1280]{3,2,0,1:T(8,128)(2,1)} %bitcast.7) | data formatting | bytes 19660800 | tf_op jit(solution)/shard_map/reshape | solution.py:51
  163.5 20.9 %copy.22 = bf16[4,1280,1280]{1,2,0:T(8,128)(2,1)} copy(bf16[4,1280,1280]{2,0,1:T(4,128)(2,1)} %all-gather.2.cloned.1.call-done) | data formatting | bytes 26214400 | tf_op jit(solution)/shard_map/all_gather | solution.py:39
  184.4 6.3 %bitcast_multiply_fusion = bf16[4,1280,1280]{1,2,0:T(8,128)(2,1)S(1)} fusion(bf16[4,1280,1280]{1,2,0:T(8,128)(2,1)} %copy.22, bf16[4,1280,20]{1,2,0:T(8,128)(2,1)S(1)} %fusion.10), kind=kLoop, calls=%fused_computation.2 | loop fusion | flops 6553600 | bytes 26419200 | tf_op jit(solution)/shard_map/mul | solution.py:18
  190.7 15.0 %fusion.1.clone.4 = bf16[3,4,320,1280]{3,2,0,1:T(8,128)(2,1)} fusion(bf16[4,1280,1280]{1,2,0:T(8,128)(2,1)S(1)} %bitcast_multiply_fusion, bf16[3,320,1280]{2,1,0:T(8,128)(2,1)S(1)} %copy-done.4), kind=kOutput, calls=%fused_computation.3.clone.clone.clone.1 | convolution fusion | flops 12587827200 | bytes 25395200 | tf_op jit(solution)/shard_map/qac,pcd->qpad/dot_general | solution.py:41
  205.7 21.9 %fusion.7 = f32[4,320,1280,1]{1,2,3,0:T(8,128)} fusion(bf16[3,1280,1280,1]{2,1,0,3:T(8,128)(2,1)} %bitcast.68, bf16[3,4,320,1280]{3,2,0,1:T(8,128)(2,1)} %fusion.1.clone.4), kind=kOutput, calls=%fused_computation.7 | convolution fusion | flops 12582912000 | bytes 26214400 | tf_op jit(solution)/shard_map/qpad,qbd->pab/dot_general | solution.py:48
  227.6 14.8 %bitcast_add_fusion = f32[4,320,1280]{1,2,0:T(8,128)} fusion(f32[4,320,1280,1]{1,2,3,0:T(8,128)} %fusion.7, bf16[4,1280,1280]{1,2,0:T(8,128)(2,1)} %copy-done.2, bf16[3,4,1280]{2,1,0:T(4,128)(2,1)S(1)} %fusion.11, bf16[3,4,320]{2,1,0:T(4,128)(2,1)S(1)} %dynamic-slice_bitcast_fusion), kind=kOutput, calls=%fused_computation.4 | convolution fusion | flops 50790400 | bytes 26252800 | tf_op jit(solution)/shard_map/qpa,qpb->pab/dot_general | solution.py:56
  242.4 90.7 %reduce-scatter.2.cloned.1.call-done = f32[4,320,40]{1,2,0:T(8,128)} async-done(((f32[4,320,1280]{1,2,0:T(8,128)}), f32[4,320,40]{1,2,0:T(8,128)}) %reduce-scatter.2.cloned.1.call-update) | async-done | bytes 204816 | tf_op jit(solution)/shard_map/reduce_scatter | solution.py:57
  (19 shorter events, 0.1 us)
Async XLA Ops:
  6.5 16.7 %copy-start = (bf16[3,160,1280]{2,1,0:T(8,128)(2,1)S(1)}, bf16[3,160,1280]{2,1,0:T(8,128)(2,1)}, u32[]{:S(2)}) copy-start(bf16[3,160,1280]{2,1,0:T(8,128)(2,1)} %param.8) | copy-start | bytes 3686404
  6.5 157.0 %all-gather.2.cloned.1.call-start = ((), (), s32[]{:S(2)}) async-start(), calls=%async_computation.2 | async-start | bytes 13209600 | tf_op jit(solution)/shard_map/all_gather | solution.py:39
  10.9 1.4 copy-start.3
  17.0 6.1 %copy-start.5 = (s32[4,20,20]{2,0,1:T(4,128)S(1)}, s32[4,20,20]{2,0,1:T(4,128)}, u32[]{:S(2)}) copy-start(s32[4,20,20]{2,0,1:T(4,128)} %param.10) | copy-start | bytes 19204
  17.0 6.2 %copy-start.6 = (s32[4,2]{0,1:T(2,128)S(1)}, s32[4,2]{0,1:T(2,128)}, u32[]{:S(2)}) copy-start(s32[4,2]{0,1:T(2,128)} %param.9) | copy-start | bytes 100
  17.0 138.3 %all-to-all-start = ((bf16[4,3,320,1280]{3,2,1,0:T(8,128)(2,1)}), bf16[4,3,320,1280]{3,2,1,0:T(8,128)(2,1)}, u32[]{:S(2)}, u32[]{:S(2)}) async-start(bf16[4,3,320,1280]{3,2,1,0:T(8,128)(2,1)} %stack.2), calls=%async_computation | async-start | bytes 19660800 | tf_op jit(solution)/shard_map/all_to_all | solution.py:52
  23.1 310.0 %reduce-scatter.2.cloned.1.call-start = ((), (), s32[]{:S(2)}) async-start(), calls=%async_computation.3 | async-start | bytes 8110080 | tf_op jit(solution)/shard_map/reduce_scatter | solution.py:57
  184.4 6.3 %copy-start.4 = (bf16[3,320,1280]{2,1,0:T(8,128)(2,1)S(1)}, bf16[3,320,1280]{2,1,0:T(8,128)(2,1)}, u32[]{:S(2)}) copy-start(bf16[3,320,1280]{2,1,0:T(8,128)(2,1)} %copy-done.3) | copy-start | bytes 7372804
  190.7 15.0 %copy-start.2 = (bf16[4,1280,1280]{1,2,0:T(8,128)(2,1)}, bf16[4,1280,1280]{1,2,0:T(8,128)(2,1)S(1)}, u32[]{:S(2)}) copy-start(bf16[4,1280,1280]{1,2,0:T(8,128)(2,1)S(1)} %bitcast_multiply_fusion) | copy-start | bytes 39321604
  227.6 105.5 %copy-start.1 = (bf16[3,160,1280]{2,1,0:T(8,128)(2,1)S(1)}, bf16[3,160,1280]{2,1,0:T(8,128)(2,1)}, u32[]{:S(2)}) copy-start(bf16[3,160,1280]{2,1,0:T(8,128)(2,1)} %param.8) | copy-start | bytes 3686404
Sparse Core Ops, SparseCore 0:
  10.3 95.2 all-gather.1
  242.6 90.5 reduce-scatter.1
